TPU v7x, 128 devices: a whole 4x4x4 slice. The times are simulated.
128 devices in a mesh: seq: 16 (over x_lo, z, core), tp: 8 (over y, x_hi).
Axes of the slice: x: 4 (x_hi: 2, x_lo: 2; x = x_hi * 2 + x_lo), y: 4, z: 4, core: 2. Of those that a mesh axis runs over, the one named last changes fastest.
Arguments:
- hidden_in: bfloat16 [6144, 3584], P('seq'), may hold values from -48 to 48
- joined_inputs: bfloat16 [6144, 8192], P('seq', 'tp'), may hold values from -64 to 64
- lengths: int32 [4], replicated, may hold values from 1 to 3072, 6144 in all
- o_weight: bfloat16 [4096, 3584], P('tp'), may hold values from -0.09375 to 0.09375
- gate_up: float32 [2, 3584, 7168], P(None, ('seq', 'tp')), may hold values from -0.09375 to 0.09375
- down_weight: bfloat16 [7168, 3584], P('tp'), may hold values from -0.0625 to 0.0625
- next_weight: bfloat16 [3584, 8192], P(None, 'tp'), may hold values from -0.09375 to 0.09375
- post_attn_gain: float32 [3584], replicated, may hold values from 0.1 to 1.9
- pre_ffw_gain: float32 [3584], replicated, may hold values from 0.1 to 1.9
- post_ffw_gain: float32 [3584], replicated, may hold values from 0.1 to 1.9
- next_gain: float32 [3584], replicated, may hold values from 0.1 to 1.9
Outputs:
- next_qkv: bfloat16 [6144, 8192], P('seq', 'tp')
Inputs may be any that keep to these rules, and one draw needn't show every extreme that they name: The lengths of 4 prompts laid end to end; they sum to 6144 and the longest is exactly 3072.
All inputs are finite; a program needn't handle non-finite values.
Results may differ from a plain program's by a relative error of at most 0.022.
Values may be sent and summed in bfloat16 or wider, within the bound.
A program may use at most 192 MiB of HBM per device.

v0:
```python
import jax
import jax.numpy as jnp
from jax import lax
from jax.sharding import PartitionSpec as P

HEADS = 16
KV_HEADS = 8
HEAD_DIM = 256


def rms_norm(values, gain):
    meansq = jnp.mean(values * values, axis=-1, keepdims=True)
    return values * lax.rsqrt(meansq + 1e-06) * gain


def local(
    hidden_in,
    joined_inputs,
    lengths,
    o_weight,
    gate_up,
    down_weight,
    next_weight,
    post_attn_gain,
    pre_ffw_gain,
    post_ffw_gain,
    next_gain,
):
    seq_count = lax.axis_size("seq")
    tp_count = lax.axis_size("tp")
    row_count = hidden_in.shape[0]
    model_width = hidden_in.shape[1]
    per_group = HEADS // KV_HEADS
    group_cols = (per_group + 2) * HEAD_DIM
    local_groups = joined_inputs.shape[1] // group_cols
    grouped = joined_inputs.reshape(row_count, local_groups, group_cols)
    queries = grouped[:, :, : per_group * HEAD_DIM].reshape(
        row_count, local_groups, per_group, HEAD_DIM
    )
    own_keys = grouped[:, :, per_group * HEAD_DIM : (per_group + 1) * HEAD_DIM]
    own_values = grouped[:, :, (per_group + 1) * HEAD_DIM :]
    keys_all, values_all = (
        lax.all_gather(own_keys, "seq", axis=0, tiled=True),
        lax.all_gather(own_values, "seq", axis=0, tiled=True),
    )
    total_rows = keys_all.shape[0]
    seq_index = lax.axis_index("seq")
    position = seq_index * row_count
    ends = jnp.cumsum(lengths)
    places = jnp.arange(total_rows, dtype=jnp.int32)
    prompt_ids = jnp.sum((places[:, None] >= ends[None, :]).astype(jnp.int32), axis=1)
    query_place = position + jnp.arange(row_count, dtype=jnp.int32)
    query_ids = lax.dynamic_slice_in_dim(prompt_ids, position, row_count, 0)
    scale = HEAD_DIM ** (-0.5)
    scores = (
        jnp.einsum("qgrd,kgd->qgrk", queries, keys_all, preferred_element_type=jnp.float32) * scale
    )
    allowed = (
        (query_ids[:, None] == prompt_ids[None, :]) & (places[None, :] <= query_place[:, None])
    )[:, None, None, :]
    scores = jnp.where(allowed, scores, -jnp.inf)
    peak = jnp.max(scores, axis=-1, keepdims=True)
    weights = jnp.where(allowed, jnp.exp(scores - peak), 0.0)
    norm_sum = jnp.sum(weights, axis=-1)
    blended = jnp.einsum(
        "qgrk,kgd->qgrd",
        weights.astype(jnp.bfloat16),
        values_all,
        preferred_element_type=jnp.float32,
    )
    blended = blended / norm_sum[..., None]
    attended = blended.astype(jnp.bfloat16).reshape(row_count, local_groups * per_group * HEAD_DIM)
    projected = jnp.dot(attended, o_weight, preferred_element_type=jnp.float32)

    def total_of(values):
        return lax.psum(values.astype(jnp.bfloat16), "tp").astype(jnp.float32)

    residual_mid = hidden_in.astype(jnp.float32) + rms_norm(total_of(projected), post_attn_gain)
    ffw_in = rms_norm(residual_mid, pre_ffw_gain).astype(jnp.bfloat16)
    server_low = gate_up.astype(jnp.bfloat16)
    stacked_rows = lax.all_gather(server_low, "seq", axis=1, tiled=True)
    local_units = lax.all_to_all(stacked_rows, "tp", split_axis=2, concat_axis=1, tiled=True)
    piece_rows = gate_up.shape[1]
    reordered = (
        ffw_in.reshape(row_count, seq_count, tp_count, piece_rows)
        .transpose(0, 2, 1, 3)
        .reshape(row_count, model_width)
    )
    gate = jnp.dot(reordered, local_units[0], preferred_element_type=jnp.float32)
    up_part = jnp.dot(reordered, local_units[1], preferred_element_type=jnp.float32)
    activated = (jax.nn.gelu(gate, approximate=True) * up_part).astype(jnp.bfloat16)
    ffw_out = jnp.dot(activated, down_weight, preferred_element_type=jnp.float32)
    residual_out = residual_mid + rms_norm(total_of(ffw_out), post_ffw_gain)
    next_in = rms_norm(residual_out, next_gain).astype(jnp.bfloat16)
    return jnp.dot(next_in, next_weight, preferred_element_type=jnp.float32).astype(jnp.bfloat16)


def solution(mesh):
    in_specs = (
        P("seq", None),
        P("seq", "tp"),
        P(),
        P("tp", None),
        P(None, ("seq", "tp"), None),
        P("tp", None),
        P(None, "tp"),
        P(),
        P(),
        P(),
        P(),
    )
    out_specs = P("seq", "tp")
    return jax.shard_map(local, mesh=mesh, in_specs=in_specs, out_specs=out_specs, check_vma=False)
```

profile of v0, /device:TPU:1, one launch (start us, length us, event | category | flops | bytes accessed | tf_op | source)
XLA Modules:
  0.0 658.8 jit_solution(18442453555862474000)
XLA Ops:
  6.5 0.0 all-gather.8.cloned.1.call-start
  6.5 2.9 convert_element_type.50
  9.4 0.0 all-gather.8.cloned.1.call-update
  9.4 0.0 all-gather.4.cloned.1.call-start
  9.5 1.8 fusion.53
  11.3 0.0 all-gather.4.cloned.1.call-update
  11.3 0.0 all-gather.6.cloned.1.call-start
  11.4 0.7 all-gather.6.cloned.1.call-update
  12.1 1.0 slice.23
  13.1 0.8 reduce-window.8
  13.9 0.2 copy.49
  14.1 0.1 convert_reduce_fusion
  14.3 0.1 dynamic_slice.3
  14.4 72.0 %all-gather.8.cloned.1.call-done = bf16[2,448,7168]{2,0,1:T(2,128)(2,1)} async-done(((bf16[2,28,7168]{2,0,1:T(2,128)(2,1)}), bf16[2,448,7168]{2,0,1:T(2,128)(2,1)}) %all-gather.8.cloned.1.call-update) | async-done | bytes 12845072 | tf_op jit(solution)/shard_map/all_gather | solution.py:81
  86.4 48.5 %copy.55 = bf16[2,448,7168]{1,0,2:T(2,128)(2,1)} copy(bf16[2,448,7168]{2,0,1:T(2,128)(2,1)} %all-gather.8.cloned.1.call-done) | data formatting | bytes 25690112 | tf_op jit(solution)/shard_map/all_gather | solution.py:81
  134.9 6.5 all-to-all-start
  141.4 0.0 all-reduce.3.cloned.1.call-start
  141.5 3.8 fusion.6
  145.2 0.0 all-gather.4.cloned.1.call-done
  145.2 5.4 fusion
  150.7 0.0 copy-start.2
  150.7 6.5 copy-done.2
  157.2 6.1 fusion.1
  163.3 4.7 all-gather.6.cloned.1.call-done
  167.9 0.0 copy-start.4
  167.9 13.2 %fusion.39 = bf16[1,256,384,2]{2,1,3,0:T(8,128)(2,1)S(1)} fusion(bf16[6144,1,256]{2,0,1:T(8,128)(2,1)} %all-gather.6.cloned.1.call-done, f32[6144,384,2]{1,0,2:T(8,128)} %copy-done.2, f32[384,2]{0,1:T(2,128)S(1)} %get-tuple-element.9, pred[384,6144]{0,1:T(8,128)(4,1)} %fusion.6, f32[384,2]{0,1:T(2,128)S(1)} %fusion.1), kind=kOutput, calls=%fused_computation.45 | convolution fusion | flops 2439905280 | bytes 24778752 | tf_op jit(solution)/shard_map/qgrk,kgd->qgrd/dot_general | solution.py:65
  181.1 0.0 copy-done.4
  181.1 0.0 copy-start.5
  181.2 3.2 convolution_convert_fusion
  184.3 0.0 copy-start.6
  184.3 0.0 all-reduce.3.cloned.1.call-update
  184.4 0.2 all-reduce.5.cloned.1.call-start
  184.6 232.3 %all-reduce.3.cloned.1.call-done = bf16[384,3584]{1,0:T(8,128)(2,1)} async-done(((bf16[384,3584]{1,0:T(8,128)(2,1)}), bf16[384,3584]{1,0:T(8,128)(2,1)}) %all-reduce.3.cloned.1.call-update) | async-done | bytes 2752528 | tf_op jit(solution)/shard_map/psum | solution.py:76
  416.9 0.0 copy-start
  416.9 2.5 fusion.8
  419.5 0.0 copy-done.5
  419.5 4.0 multiply_reduce_fusion.1
  423.5 0.0 copy-done.6
  423.5 0.0 copy-done
  423.5 5.1 multiply_convert_fusion.1
  428.7 4.5 copy.53
  433.2 5.2 reshape.159
  438.4 4.0 copy.54
  442.4 5.2 reshape.160
  447.6 0.0 all-to-all-done
  447.6 24.5 %copy.63 = bf16[2,448,8,896]{3,2,1,0:T(8,128)(2,1)} copy(bf16[2,448,8,896]{1,0,3,2:T(2,128)(2,1)} %bitcast.16) | data formatting | bytes 25690112 | tf_op jit(solution)/shard_map/all_to_all | solution.py:82
  472.1 8.3 %fusion.52 = (bf16[1,8,448,896]{3,1,2,0:T(8,128)(2,1)}, bf16[1,8,448,896]{3,1,2,0:T(8,128)(2,1)S(1)}) fusion(bf16[2,8,448,896]{3,1,2,0:T(8,128)(2,1)} %bitcast.80), kind=kLoop, calls=%fused_computation.60 | loop fusion | bytes 25690112 | tf_op jit(solution)/shard_map/slice | solution.py:89
  480.4 3.9 copy.57
  484.3 3.8 copy.58
  488.1 5.9 fusion.54
  494.0 13.5 %convolution_convert_fusion.1 = bf16[384,3584]{1,0:T(8,128)(2,1)} fusion(bf16[896,3584]{1,0:T(8,128)(2,1)} %param.16, bf16[384,3584]{0,1:T(8,128)(2,1)} %reshape.160, bf16[3584,896]{1,0:T(8,128)(2,1)} %bitcast.83, f32[384,896]{1,0:T(8,128)} %fusion.54), kind=kOutput, calls=%fused_computation.15 | convolution fusion | flops 4937318400 | bytes 19726336 | tf_op jit(solution)/shard_map/dot_general | solution.py:92
  507.4 0.0 copy-start.7
  507.4 0.0 all-reduce.5.cloned.1.call-update
  507.5 0.0 copy-start.8
  507.5 129.4 %all-reduce.5.cloned.1.call-done = bf16[384,3584]{1,0:T(8,128)(2,1)} async-done(((bf16[384,3584]{1,0:T(8,128)(2,1)}), bf16[384,3584]{1,0:T(8,128)(2,1)}) %all-reduce.5.cloned.1.call-update) | async-done | bytes 2752528 | tf_op jit(solution)/shard_map/psum | solution.py:76
  636.9 0.0 copy-start.1
  636.9 0.0 copy-start.3
  636.9 2.5 fusion.11
  639.5 0.0 copy-done.7
  639.5 4.8 multiply_reduce_fusion
  644.3 0.0 copy-done.8
  644.3 0.0 copy-done.1
  644.3 0.0 copy-done.3
  644.3 8.0 %fusion.20 = bf16[384,1024]{1,0:T(8,128)(2,1)} fusion(bf16[3584,1024]{1,0:T(8,128)(2,1)} %param.17, f32[3584]{0:T(1024)S(1)} %copy-done.8, f32[384]{0:T(512)S(1)} %add_rsqrt_fusion, bf16[384,3584]{1,0:T(8,128)(2,1)S(1)} %copy-done.3, bf16[384,3584]{1,0:T(8,128)(2,1)S(1)} %copy-done, bf16[384,3584]{1,0:T(8,128)(2,1)S(1)} %copy-done.1, ...), kind=kOutput, calls=%fused_computation.34 | convolution fusion | flops 2835480576 | bytes 16431616 | tf_op jit(solution)/shard_map/dot_general | solution.py:95
  (5 shorter events, 0.0 us)
Async XLA Ops:
  6.5 79.8 %all-gather.8.cloned.1.call-start = ((), (), s32[]{:S(2)}) async-start(), calls=%async_computation.4 | async-start | bytes 13647872 | tf_op jit(solution)/shard_map/all_gather | solution.py:81
  9.4 135.8 %all-gather.4.cloned.1.call-start = ((), (), s32[]{:S(2)}) async-start(), calls=%async_computation.1 | async-start | bytes 3342336 | tf_op jit(solution)/shard_map/all_gather | solution.py:43
  11.3 156.6 %all-gather.6.cloned.1.call-start = ((), (), s32[]{:S(2)}) async-start(), calls=%async_computation.2 | async-start | bytes 3342336 | tf_op jit(solution)/shard_map/all_gather | solution.py:44
  134.9 312.7 %all-to-all-start = ((bf16[2,448,7168]{1,0,2:T(2,128)(2,1)}), bf16[2,448,7168]{1,0,2:T(2,128)(2,1)}, u32[]{:S(2)}, u32[]{:S(2)}) async-start(bf16[2,448,7168]{1,0,2:T(2,128)(2,1)} %copy.55), calls=%async_computation | async-start | bytes 29360128 | tf_op jit(solution)/shard_map/all_to_all | solution.py:82
  141.4 275.5 %all-reduce.3.cloned.1.call-start = ((), (), s32[]{:S(2)}) async-start(), calls=%async_computation.3 | async-start | bytes 5505024 | tf_op jit(solution)/shard_map/psum | solution.py:76
  150.7 6.5 copy-start.2
  167.9 13.2 %copy-start.4 = (bf16[512,3584]{1,0:T(8,128)(2,1)S(1)}, bf16[512,3584]{1,0:T(8,128)(2,1)}, u32[]{:S(2)}) copy-start(bf16[512,3584]{1,0:T(8,128)(2,1)} %param.14) | copy-start | bytes 11010052
  181.1 238.4 %copy-start.5 = (f32[3584]{0:T(1024)S(1)}, f32[3584]{0:T(1024)}, u32[]{:S(2)}) copy-start(f32[3584]{0:T(1024)} %param.18) | copy-start | bytes 43012
  184.3 239.2 %copy-start.6 = (f32[3584]{0:T(1024)S(1)}, f32[3584]{0:T(1024)}, u32[]{:S(2)}) copy-start(f32[3584]{0:T(1024)} %param.19) | copy-start | bytes 43012
  184.4 452.5 %all-reduce.5.cloned.1.call-start = ((), (), s32[]{:S(2)}) async-start(), calls=%async_computation.5 | async-start | bytes 5505024 | tf_op jit(solution)/shard_map/psum | solution.py:76
  416.9 6.6 copy-start
  507.4 132.0 %copy-start.7 = (f32[3584]{0:T(1024)S(1)}, f32[3584]{0:T(1024)}, u32[]{:S(2)}) copy-start(f32[3584]{0:T(1024)} %param.20) | copy-start | bytes 43012
  507.5 136.8 %copy-start.8 = (f32[3584]{0:T(1024)S(1)}, f32[3584]{0:T(1024)}, u32[]{:S(2)}) copy-start(f32[3584]{0:T(1024)} %param.21) | copy-start | bytes 43012
  636.9 7.4 %copy-start.1 = (bf16[384,3584]{1,0:T(8,128)(2,1)S(1)}, bf16[384,3584]{1,0:T(8,128)(2,1)}, u32[]{:S(2)}) copy-start(bf16[384,3584]{1,0:T(8,128)(2,1)} %param.11) | copy-start | bytes 8257540
  636.9 7.4 %copy-start.3 = (bf16[384,3584]{1,0:T(8,128)(2,1)S(1)}, bf16[384,3584]{1,0:T(8,128)(2,1)}, u32[]{:S(2)}) copy-start(bf16[384,3584]{1,0:T(8,128)(2,1)} %all-reduce.5.cloned.1.call-done) | copy-start | bytes 8257540
Sparse Core Ops, SparseCore 0:
  9.6 76.7 all-gather.7
  88.1 37.0 all-gather.3
  126.8 41.0 all-gather.5
  184.5 232.4 all-reduce.2
  507.6 129.2 all-reduce.4
where the time goes:
time: 662 us; the launch traced here: 659 us
  waiting for transfers between devices  439 us (66%)
  local copies, waits for them, and re-layouts  118 us (18%)
  matrix products  49.1 us (7%)
  other arithmetic  32.8 us (5%)
  between operations  13.3 us (2%)
  starting transfers between devices  6.85 us (1%)
    psum x2, waiting for transfers between devices, total_of(): return lax.psum(values.astype(jnp.bfloat16), 'tp').astype(jnp.float32)  362 us
    all_gather x1, waiting for transfers between devices, local(): stacked_rows = lax.all_gather(server_low, 'seq', axis=1, tiled=True)  72 us
    all_gather x1, local copies, waits for them, and re-layouts, local(): stacked_rows = lax.all_gather(server_low, 'seq', axis=1, tiled=True)  48.5 us
    all_to_all x1, local copies, waits for them, and re-layouts, local(): lax.all_to_all(stacked_rows, 'tp', split_axis=2, concat_axis=1, tiled=True)  24.5 us
    reduce_sum x4, other arithmetic, rms_norm(): meansq = jnp.mean(values * values, axis=-1, keepdims=True)  13.9 us
    dot_general x1, matrix products, local(): jnp.dot(activated, down_weight, preferred_element_type=jnp.float32)  13.5 us
  transfers between devices with their start and end apart: 6, of which 4 were waited for; matrix products, arithmetic and copies ran while one was open for 17% of the time, Pallas kernels for 0%

commit v1 on v0

--- a/solution.py
+++ b/solution.py
@@ -78,7 +78,8 @@
     residual_mid = hidden_in.astype(jnp.float32) + rms_norm(total_of(projected), post_attn_gain)
     ffw_in = rms_norm(residual_mid, pre_ffw_gain).astype(jnp.bfloat16)
     server_low = gate_up.astype(jnp.bfloat16)
-    stacked_rows = lax.all_gather(server_low, "seq", axis=1, tiled=True)
+    stack = jnp.stack([server_low] * lax.axis_size("seq"))
+    stacked_rows = jnp.concatenate(lax.all_to_all(stack, "seq", 0, 0), axis=1)
     local_units = lax.all_to_all(stacked_rows, "tp", split_axis=2, concat_axis=1, tiled=True)
     piece_rows = gate_up.shape[1]
     reordered = (

time: 662 us -> 782 us (1.18)
  waiting for transfers between devices: 439 us -> 547 us
    all_to_all x0 -> x1, waiting for transfers between devices: none -> 188 us  [local(): stacked_rows = jnp.concatenate(lax.all_to_all(stack, 'seq', 0, 0), axis=1)]
    all_gather x1 -> x0, waiting for transfers between devices: 72 us -> none  [local(): stacked_rows = lax.all_gather(server_low, 'seq', axis=1, tiled=True)]
    reshape x0 -> x1, local copies, waits for them, and re-layouts: none -> 48.5 us  [local(): stacked_rows = jnp.concatenate(lax.all_to_all(stack, 'seq', 0, 0), axis=1)]
    all_gather x1 -> x0, local copies, waits for them, and re-layouts: 48.5 us -> none  [local(): stacked_rows = lax.all_gather(server_low, 'seq', axis=1, tiled=True)]
    another operation x0 -> x1, local copies, waits for them, and re-layouts: none -> 8.52 us  [local(): stack = jnp.stack([server_low] * lax.axis_size('seq'))]
    all_to_all x0 -> x1, starting transfers between devices: none -> 7.89 us  [local(): stacked_rows = jnp.concatenate(lax.all_to_all(stack, 'seq', 0, 0), axis=1)]
  transfers between devices with their start and end apart: 6 -> 6, of which waited for: 4 -> 3; matrix products, arithmetic and copies ran while one was open for 17% -> 14% of each run, Pallas kernels for 0% -> 0%
where the time goes in v1:
time: 782 us; the launch traced here: 779 us
  waiting for transfers between devices  547 us (70%)
  local copies, waits for them, and re-layouts  124 us (16%)
  matrix products  49.1 us (6%)
  other arithmetic  31.2 us (4%)
  starting transfers between devices  14.4 us (2%)
  between operations  13.3 us (2%)
    psum x2, waiting for transfers between devices, total_of(): return lax.psum(values.astype(jnp.bfloat16), 'tp').astype(jnp.float32)  358 us
    all_to_all x1, waiting for transfers between devices, local(): stacked_rows = jnp.concatenate(lax.all_to_all(stack, 'seq', 0, 0), axis=1)  188 us
    reshape x1, local copies, waits for them, and re-layouts, local(): stacked_rows = jnp.concatenate(lax.all_to_all(stack, 'seq', 0, 0), axis=1)  48.5 us
    all_to_all x1, local copies, waits for them, and re-layouts, local(): lax.all_to_all(stacked_rows, 'tp', split_axis=2, concat_axis=1, tiled=True)  24.5 us
  transfers between devices with their start and end apart: 6, of which 3 were waited for; matrix products, arithmetic and copies ran while one was open for 14% of the time, Pallas kernels for 0%

profile of v1, /device:TPU:1, one launch (start us, length us, event | category | flops | bytes accessed | tf_op | source)
XLA Modules:
  0.0 779.3 jit_solution(4079607886459341114)
XLA Ops:
  6.5 2.0 convert_element_type.50
  8.5 8.5 %stack.2 = bf16[16,2,28,7168]{3,1,2,0:T(2,128)(2,1)} broadcast(bf16[2,28,7168]{2,0,1:T(2,128)(2,1)S(1)} %convert_element_type.50), dimensions={1,2,3} | broadcast | bytes 13647872 | tf_op jit(solution)/shard_map/stack | solution.py:81
  17.0 0.0 copy-start.5
  17.0 0.0 copy-start.10
  17.0 7.9 %all-to-all-start = ((bf16[16,2,28,7168]{3,1,2,0:T(2,128)(2,1)}), bf16[16,2,28,7168]{3,1,2,0:T(2,128)(2,1)}, u32[]{:S(2)}, u32[]{:S(2)}) async-start(bf16[16,2,28,7168]{3,1,2,0:T(2,128)(2,1)} %stack.2), calls=%async_computation | async-start | bytes 25690112 | tf_op jit(solution)/shard_map/all_to_all | solution.py:82
  24.9 0.0 all-gather.3.cloned.1.call-start
  25.0 0.0 copy-done.5
  25.0 0.8 fusion.53
  25.8 0.0 all-gather.3.cloned.1.call-update
  25.8 0.0 all-gather.5.cloned.1.call-start
  25.8 0.7 all-gather.5.cloned.1.call-update
  26.6 0.0 copy-done.10
  26.6 0.2 reduce-window.8
  26.8 0.2 copy.49
  27.0 0.1 convert_reduce_fusion
  27.1 0.1 dynamic_slice.3
  27.2 188.3 %all-to-all-done = bf16[16,2,28,7168]{3,1,2,0:T(2,128)(2,1)} async-done(((bf16[16,2,28,7168]{3,1,2,0:T(2,128)(2,1)}), bf16[16,2,28,7168]{3,1,2,0:T(2,128)(2,1)}, u32[]{:S(2)}, u32[]{:S(2)}) %all-to-all-start) | async-done | bytes 12845088 | tf_op jit(solution)/shard_map/all_to_all | solution.py:82
  215.6 48.5 %copy.55 = bf16[2,448,7168]{1,0,2:T(2,128)(2,1)} copy(bf16[2,448,7168]{2,0,1:T(2,128)(2,1)} %bitcast.17) | data formatting | bytes 25690112 | tf_op jit(solution)/shard_map/reshape | solution.py:82
  264.1 6.1 all-to-all-start.1
  270.3 0.0 all-reduce.3.cloned.1.call-start
  270.3 3.8 fusion.6
  274.1 0.0 all-gather.3.cloned.1.call-done
  274.1 5.4 fusion
  279.5 0.0 copy-start.2
  279.5 6.5 copy-done.2
  286.0 6.1 fusion.1
  292.1 0.0 all-gather.5.cloned.1.call-done
  292.1 0.0 copy-start.4
  292.1 13.2 %fusion.39 = bf16[1,256,384,2]{2,1,3,0:T(8,128)(2,1)S(1)} fusion(bf16[6144,1,256]{2,0,1:T(8,128)(2,1)} %all-gather.5.cloned.1.call-done, f32[6144,384,2]{1,0,2:T(8,128)} %copy-done.2, f32[384,2]{0,1:T(2,128)S(1)} %get-tuple-element.9, pred[384,6144]{0,1:T(8,128)(4,1)} %fusion.6, f32[384,2]{0,1:T(2,128)S(1)} %fusion.1), kind=kOutput, calls=%fused_computation.45 | convolution fusion | flops 2439905280 | bytes 24778752 | tf_op jit(solution)/shard_map/qgrk,kgd->qgrd/dot_general | solution.py:65
  305.3 0.0 copy-done.4
  305.3 0.0 copy-start.6
  305.3 3.2 convolution_convert_fusion
  308.5 0.0 copy-start.7
  308.5 0.0 all-reduce.3.cloned.1.call-update
  308.6 0.2 all-reduce.5.cloned.1.call-start
  308.8 228.1 %all-reduce.3.cloned.1.call-done = bf16[384,3584]{1,0:T(8,128)(2,1)} async-done(((bf16[384,3584]{1,0:T(8,128)(2,1)}), bf16[384,3584]{1,0:T(8,128)(2,1)}) %all-reduce.3.cloned.1.call-update) | async-done | bytes 2752528 | tf_op jit(solution)/shard_map/psum | solution.py:76
  536.9 0.0 copy-start
  536.9 2.5 fusion.8
  539.4 0.0 copy-done.6
  539.4 4.0 multiply_reduce_fusion.1
  543.4 0.0 copy-done.7
  543.5 0.0 copy-done
  543.5 5.1 multiply_convert_fusion.1
  548.6 4.5 copy.53
  553.1 5.2 reshape.167
  558.3 4.0 copy.54
  562.4 5.2 reshape.168
  567.6 0.0 all-to-all-done.1
  567.6 24.5 %copy.63 = bf16[2,448,8,896]{3,2,1,0:T(8,128)(2,1)} copy(bf16[2,448,8,896]{1,0,3,2:T(2,128)(2,1)} %bitcast.18) | data formatting | bytes 25690112 | tf_op jit(solution)/shard_map/all_to_all | solution.py:83
  592.1 8.3 %fusion.52 = (bf16[1,8,448,896]{3,1,2,0:T(8,128)(2,1)}, bf16[1,8,448,896]{3,1,2,0:T(8,128)(2,1)S(1)}) fusion(bf16[2,8,448,896]{3,1,2,0:T(8,128)(2,1)} %bitcast.83), kind=kLoop, calls=%fused_computation.60 | loop fusion | bytes 25690112 | tf_op jit(solution)/shard_map/slice | solution.py:90
  600.3 3.9 copy.57
  604.2 3.8 copy.58
  608.0 5.9 fusion.54
  613.9 13.4 %convolution_convert_fusion.1 = bf16[384,3584]{1,0:T(8,128)(2,1)} fusion(bf16[896,3584]{1,0:T(8,128)(2,1)} %param.16, bf16[384,3584]{0,1:T(8,128)(2,1)} %reshape.168, bf16[3584,896]{1,0:T(8,128)(2,1)} %bitcast.86, f32[384,896]{1,0:T(8,128)} %fusion.54), kind=kOutput, calls=%fused_computation.15 | convolution fusion | flops 4937318400 | bytes 19726336 | tf_op jit(solution)/shard_map/dot_general | solution.py:93
  627.4 0.0 all-reduce.5.cloned.1.call-update
  627.4 0.0 copy-start.9
  627.4 130.0 %all-reduce.5.cloned.1.call-done = bf16[384,3584]{1,0:T(8,128)(2,1)} async-done(((bf16[384,3584]{1,0:T(8,128)(2,1)}), bf16[384,3584]{1,0:T(8,128)(2,1)}) %all-reduce.5.cloned.1.call-update) | async-done | bytes 2752528 | tf_op jit(solution)/shard_map/psum | solution.py:76
  757.4 2.5 fusion.11
  759.9 0.0 copy-done.8
  759.9 4.8 multiply_reduce_fusion
  764.7 0.0 copy-done.9
  764.8 0.0 copy-done.1
  764.8 0.0 copy-done.3
  764.8 8.0 %fusion.20 = bf16[384,1024]{1,0:T(8,128)(2,1)} fusion(bf16[3584,1024]{1,0:T(8,128)(2,1)} %param.17, f32[3584]{0:T(1024)S(1)} %copy-done.9, f32[384]{0:T(512)S(1)} %add_rsqrt_fusion, bf16[384,3584]{1,0:T(8,128)(2,1)S(1)} %copy-done.3, bf16[384,3584]{1,0:T(8,128)(2,1)S(1)} %copy-done, bf16[384,3584]{1,0:T(8,128)(2,1)S(1)} %copy-done.1, ...), kind=kOutput, calls=%fused_computation.34 | convolution fusion | flops 2835480576 | bytes 16431616 | tf_op jit(solution)/shard_map/dot_general | solution.py:96
  (9 shorter events, 0.1 us)
Async XLA Ops:
  17.0 7.9 %copy-start.5 = (bf16[384,1024]{1,0:T(8,128)(2,1)S(1)}, bf16[384,1024]{1,0:T(8,128)(2,1)}, u32[]{:S(2)}) copy-start(bf16[384,1024]{1,0:T(8,128)(2,1)} %param.12) | copy-start | bytes 2359300
  17.0 9.6 %copy-start.10 = (s32[4]{0:T(128)S(1)}, s32[4]{0:T(128)}, u32[]{:S(2)}) copy-start(s32[4]{0:T(128)} %param.13) | copy-start | bytes 52
  17.0 198.5 %all-to-all-start = ((bf16[16,2,28,7168]{3,1,2,0:T(2,128)(2,1)}), bf16[16,2,28,7168]{3,1,2,0:T(2,128)(2,1)}, u32[]{:S(2)}, u32[]{:S(2)}) async-start(bf16[16,2,28,7168]{3,1,2,0:T(2,128)(2,1)} %stack.2), calls=%async_computation | async-start | bytes 25690112 | tf_op jit(solution)/shard_map/all_to_all | solution.py:82
  24.9 249.2 %all-gather.3.cloned.1.call-start = ((), (), s32[]{:S(2)}) async-start(), calls=%async_computation.2 | async-start | bytes 3342336 | tf_op jit(solution)/shard_map/all_gather | solution.py:43
  25.8 266.3 %all-gather.5.cloned.1.call-start = ((), (), s32[]{:S(2)}) async-start(), calls=%async_computation.3 | async-start | bytes 3342336 | tf_op jit(solution)/shard_map/all_gather | solution.py:44
  264.1 303.5 %all-to-all-start.1 = ((bf16[2,448,7168]{1,0,2:T(2,128)(2,1)}), bf16[2,448,7168]{1,0,2:T(2,128)(2,1)}, u32[]{:S(2)}, u32[]{:S(2)}) async-start(bf16[2,448,7168]{1,0,2:T(2,128)(2,1)} %copy.55), calls=%async_computation.1 | async-start | bytes 29360128 | tf_op jit(solution)/shard_map/all_to_all | solution.py:83
  270.3 266.6 %all-reduce.3.cloned.1.call-start = ((), (), s32[]{:S(2)}) async-start(), calls=%async_computation.4 | async-start | bytes 5505024 | tf_op jit(solution)/shard_map/psum | solution.py:76
  279.5 6.5 copy-start.2
  292.1 13.2 %copy-start.4 = (bf16[512,3584]{1,0:T(8,128)(2,1)S(1)}, bf16[512,3584]{1,0:T(8,128)(2,1)}, u32[]{:S(2)}) copy-start(bf16[512,3584]{1,0:T(8,128)(2,1)} %param.14) | copy-start | bytes 11010052
  305.3 234.1 %copy-start.6 = (f32[3584]{0:T(1024)S(1)}, f32[3584]{0:T(1024)}, u32[]{:S(2)}) copy-start(f32[3584]{0:T(1024)} %param.18) | copy-start | bytes 43012
  308.5 234.9 %copy-start.7 = (f32[3584]{0:T(1024)S(1)}, f32[3584]{0:T(1024)}, u32[]{:S(2)}) copy-start(f32[3584]{0:T(1024)} %param.19) | copy-start | bytes 43012
  308.6 448.8 %all-reduce.5.cloned.1.call-start = ((), (), s32[]{:S(2)}) async-start(), calls=%async_computation.5 | async-start | bytes 5505024 | tf_op jit(solution)/shard_map/psum | solution.py:76
  536.9 6.6 copy-start
  627.3 132.6 %copy-start.8 = (f32[3584]{0:T(1024)S(1)}, f32[3584]{0:T(1024)}, u32[]{:S(2)}) copy-start(f32[3584]{0:T(1024)} %param.20) | copy-start | bytes 43012
  627.4 137.4 %copy-start.9 = (f32[3584]{0:T(1024)S(1)}, f32[3584]{0:T(1024)}, u32[]{:S(2)}) copy-start(f32[3584]{0:T(1024)} %param.21) | copy-start | bytes 43012
  757.4 7.4 copy-start.1
  757.4 7.4 copy-start.3
Sparse Core Ops, SparseCore 0:
  27.5 146.7 all-gather.2
  175.9 60.0 all-gather.4
  308.7 228.1 all-reduce.2
  627.5 129.8 all-reduce.4
